TPU v7x, 128 devices: a whole 4x4x4 slice. The times are simulated.
128 devices in a mesh: ap: 16 (over z_lo, y, core), sc: 8 (over z_hi, x).
Axes of the slice: x: 4, y: 4, z: 4 (z_hi: 2, z_lo: 2; z = z_hi * 2 + z_lo), core: 2. Of those that a mesh axis runs over, the one named last changes fastest.
Arguments:
- observed_signal: float32 [2, 14, 128, 4, 2048], P(None, None, 'sc', None, 'ap'), may hold values from -6 to 6
- delays: float32 [4, 256, 2048], P(None, 'sc', 'ap'), may hold values from 0 to 64
- sines: float32 [4, 256, 2048], P(None, 'sc', 'ap'), may hold values from -1 to 1
- path_gain_real: float32 [4, 256, 2048], P(None, 'sc', 'ap'), may hold values from -0.078125 to 0.078125
- path_gain_imaginary: float32 [4, 256, 2048], P(None, 'sc', 'ap'), may hold values from -0.078125 to 0.078125
- counts: int32 [256, 2048], P(None, 'ap'), may hold values from 0 to 4
- regularizer: float32 [256], replicated, may hold values from 0.3 to 3
Outputs:
- estimates: float32 [2, 14, 128, 256], P(None, None, 'sc')
All inputs are finite; a program needn't handle non-finite values.
Results may differ from a plain program's by a relative error of at most 0.00038.
Values sent between devices are 32-bit elements; how exact they have to be, the bound alone decides.
No kernel may reach another device: no remote copies, remote signals or barrier semaphores. Data moves between devices by JAX's collectives and lax.ppermute only.
A program may use at most 128 MiB of HBM per device.

v0:
```python
import math

import jax
import jax.numpy as jnp
from jax import lax
from jax.sharding import PartitionSpec as P

ELEMENTS_PER_UNIT = 4
FFT_LEN = 512


def copy_for_each(value, axis):
    length = lax.axis_size(axis)
    return lax.all_to_all(
        jnp.broadcast_to(value[None], (length, *value.shape)), axis, 0, 0, tiled=True
    )


def laid_out(parts, dim):
    parts = jnp.moveaxis(parts, 0, dim)
    lengths = parts.shape
    return parts.reshape(*lengths[:dim], lengths[dim] * lengths[dim + 1], *lengths[dim + 2 :])


def gather_directly(value, axis, dim):
    parts = copy_for_each(value, axis)
    return laid_out(parts, dim)


def in_one_piece(arrays, axis, dim, along):
    widths = [a.shape[along] for a in arrays]
    both = jnp.concatenate(arrays, axis=along)
    result = gather_directly(both, axis, dim)
    return tuple(jnp.split(result, [sum(widths[:k]) for k in range(1, len(widths))], axis=along))


def sent_together(arrays, axis, dim, along):
    both = jnp.concatenate(arrays, axis=along)
    result, at, gathered = (lax.psum_scatter(both, axis, scatter_dimension=dim, tiled=True), 0, [])
    for a in arrays:
        gathered.append(lax.slice_in_dim(result, at, at + a.shape[along], axis=along))
        at += a.shape[along]
    return tuple(gathered)


def solve_one(gram_matrices, filtered_output, regularizer):
    user_index = gram_matrices.shape[1]
    shifted = gram_matrices[0] + jnp.diag(regularizer)
    system = jnp.concatenate(
        [
            jnp.concatenate([shifted, -gram_matrices[1]], 1),
            jnp.concatenate([gram_matrices[1], shifted], 1),
        ],
        0,
    )
    rhs = jnp.concatenate([filtered_output[0].T, filtered_output[1].T], 0)
    factor = jnp.linalg.cholesky(system)
    solved = jax.scipy.linalg.cho_solve((factor, True), rhs)
    return jnp.stack([solved[:user_index].T, solved[user_index:].T])


def on_device(
    observed_signal, delays, sines, path_gain_real, path_gain_imaginary, counts, regularizer
):
    tables = in_one_piece((delays, sines, path_gain_real, path_gain_imaginary), "sc", 1, 0)
    delays_all, sines_all, re_all, im_all = tables
    user_index = delays_all.shape[1]
    transmitted_data = observed_signal.shape[1]
    slots = jnp.arange(delays_all.shape[0], dtype=jnp.int32)[:, None, None]
    alive = (slots < counts[None]).astype(jnp.float32)
    weight_re = re_all * alive
    weight_im = im_all * alive
    antenna_index = jnp.arange(ELEMENTS_PER_UNIT, dtype=jnp.float32)
    steer_angle = math.pi * antenna_index[None, None, :, None] * sines_all[:, :, None, :]
    steer_cos = jnp.cos(steer_angle)
    steer_sin = jnp.sin(steer_angle)
    lead_re = weight_re[:, :, None, :] * steer_cos - weight_im[:, :, None, :] * steer_sin
    lead_im = weight_re[:, :, None, :] * steer_sin + weight_im[:, :, None, :] * steer_cos
    unit_response = observed_signal.shape[2]
    starting_shift = lax.axis_index("sc") * unit_response

    def tone_responses(tone_position):
        tone_frequency = (starting_shift + tone_position).astype(jnp.float32)
        turn = -(2.0 * math.pi / FFT_LEN) * tone_frequency * delays_all
        turn_cos = jnp.cos(turn)[:, :, None, :]
        turn_sin = jnp.sin(turn)[:, :, None, :]
        real_part = jnp.sum(lead_re * turn_cos - lead_im * turn_sin, axis=0).reshape(user_index, -1)
        imag_part = jnp.sum(lead_re * turn_sin + lead_im * turn_cos, axis=0).reshape(user_index, -1)
        stacked = jnp.concatenate([real_part, imag_part], 0)
        packed = stacked.astype(jnp.bfloat16)
        blocks = lax.dot_general(
            packed, packed, (((1,), (1,)), ((), ())), preferred_element_type=jnp.float32
        )
        gram_re = blocks[:user_index, :user_index] + blocks[user_index:, user_index:]
        gram_im = blocks[:user_index, user_index:] - blocks[user_index:, :user_index]
        measured_values = observed_signal[:, :, tone_position].reshape(2 * transmitted_data, -1)
        matched = lax.dot_general(
            stacked,
            measured_values,
            (((1,), (1,)), ((), ())),
            precision=lax.Precision.HIGHEST,
            preferred_element_type=jnp.float32,
        )
        filt_re = matched[:user_index, :transmitted_data] + matched[user_index:, transmitted_data:]
        filt_im = matched[:user_index, transmitted_data:] - matched[user_index:, :transmitted_data]
        gram_part = jnp.stack([gram_re, gram_im])
        return (gram_part, jnp.stack([filt_re.T, filt_im.T]))

    gram_matrices, filtered_output = lax.map(
        tone_responses, jnp.arange(unit_response, dtype=jnp.int32)
    )
    owned_grams, owned_filtered = sent_together((gram_matrices, filtered_output), "ap", 0, 2)
    owned = jax.vmap(solve_one, in_axes=(0, 0, None))(owned_grams, owned_filtered, regularizer)
    solution = gather_directly(owned, "ap", 0)
    return jnp.transpose(solution, (1, 2, 0, 3))


def solution(mesh):
    placed = (
        P(None, None, "sc", None, "ap"),
        P(None, "sc", "ap"),
        P(None, "sc", "ap"),
        P(None, "sc", "ap"),
        P(None, "sc", "ap"),
        P(None, "ap"),
        P(),
    )
    return jax.shard_map(
        on_device, mesh=mesh, in_specs=placed, out_specs=P(None, None, "sc", None), check_vma=False
    )
```

profile of v0, /device:TPU:0, one launch (start us, length us, event | category | flops | bytes accessed | tf_op | source)
XLA Modules:
  0.0 613.1 jit_solution(16238838982114033894)
XLA Ops:
  6.5 1.0 pad_maximum_fusion.3
  7.5 1.6 broadcast_in_dim.62
  9.1 7.7 %all-to-all-start = ((f32[8,16,32,128]{3,2,1,0:T(8,128)}), f32[8,16,32,128]{3,2,1,0:T(8,128)S(1)}, u32[]{:S(2)}, u32[]{:S(2)}) async-start(f32[8,16,32,128]{3,2,1,0:T(8,128)} %broadcast_in_dim.62), calls=%async_computation | async-start | bytes 4194304 | tf_op jit(solution)/shard_map/all_to_all | solution.py:14
  16.9 28.4 %all-to-all-done = f32[8,16,32,128]{3,2,1,0:T(8,128)S(1)} async-done(((f32[8,16,32,128]{3,2,1,0:T(8,128)}), f32[8,16,32,128]{3,2,1,0:T(8,128)S(1)}, u32[]{:S(2)}, u32[]{:S(2)}) %all-to-all-start) | async-done | bytes 2097184 | tf_op jit(solution)/shard_map/all_to_all | solution.py:14
  45.5 1.0 fusion.69
  46.5 0.9 bitcast_select_fusion
  47.4 309.2 %while.16 = (s32[]{:T(128)}, f32[16,2,256,256]{2,3,1,0:T(8,128)}, f32[16,2,14,256]{3,2,1,0:T(8,128)}, s32[16]{0:T(128)S(1)}, s32[]{:T(128)}, /*index=5*/f32[4,25...) while((s32[]{:T(128)}, f32[16,2,256,256]{2,3,1,0:T(8,128)}, ...), condition=%wide.region_3.4_spmd.clone.clone, body=%wide.region_0.3_spmd.clone.clone.sunk | while | flops 365836288 | bytes 15836415 | solution.py:109
  48.8 1.9 multiply_cosine_fusion.3
  50.7 9.7 %fusion.93 = (f32[256,4,128]{2,0,1:T(8,128)S(1)}, f32[256,4,128]{2,0,1:T(8,128)S(1)}) fusion(f32[4,256,128]{2,1,0:T(8,128)S(1)} %get-tuple-element.355, f32[4,256,128]{2,1,0:T(8,128)} %get-tuple-element.353, f32[4]{0:T(128)S(1)} %get-tuple-element.354, f32[4,256,128]{2,1,0:T(8,128)} %get-tuple-element.352, f32[4,256,128]{2,1,0:T(8,128)S(1)} %get-tuple-element.305, ...), kind=kLoop, calls=%fused_computation.15.clone.1 | loop fusion | flops 7602176 | bytes 3670032 | tf_op jit(solution)/shard_map/while/body/eval_jaxpr/reduce_sum | solution.py:87
  61.6 0.9 constant_dynamic-update-slice_fusion.6
  68.1 1.9 multiply_cosine_fusion.3
  70.0 9.7 %fusion.93 = (f32[256,4,128]{2,0,1:T(8,128)S(1)}, f32[256,4,128]{2,0,1:T(8,128)S(1)}) fusion(f32[4,256,128]{2,1,0:T(8,128)S(1)} %get-tuple-element.355, f32[4,256,128]{2,1,0:T(8,128)} %get-tuple-element.353, f32[4]{0:T(128)S(1)} %get-tuple-element.354, f32[4,256,128]{2,1,0:T(8,128)} %get-tuple-element.352, f32[4,256,128]{2,1,0:T(8,128)S(1)} %get-tuple-element.305, ...), kind=kLoop, calls=%fused_computation.15.clone.1 | loop fusion | flops 7602176 | bytes 3670032 | tf_op jit(solution)/shard_map/while/body/eval_jaxpr/reduce_sum | solution.py:87
  80.9 0.9 constant_dynamic-update-slice_fusion.6
  87.5 1.9 multiply_cosine_fusion.3
  89.4 9.7 %fusion.93 = (f32[256,4,128]{2,0,1:T(8,128)S(1)}, f32[256,4,128]{2,0,1:T(8,128)S(1)}) fusion(f32[4,256,128]{2,1,0:T(8,128)S(1)} %get-tuple-element.355, f32[4,256,128]{2,1,0:T(8,128)} %get-tuple-element.353, f32[4]{0:T(128)S(1)} %get-tuple-element.354, f32[4,256,128]{2,1,0:T(8,128)} %get-tuple-element.352, f32[4,256,128]{2,1,0:T(8,128)S(1)} %get-tuple-element.305, ...), kind=kLoop, calls=%fused_computation.15.clone.1 | loop fusion | flops 7602176 | bytes 3670032 | tf_op jit(solution)/shard_map/while/body/eval_jaxpr/reduce_sum | solution.py:87
  106.8 1.9 multiply_cosine_fusion.3
  108.7 9.7 %fusion.93 = (f32[256,4,128]{2,0,1:T(8,128)S(1)}, f32[256,4,128]{2,0,1:T(8,128)S(1)}) fusion(f32[4,256,128]{2,1,0:T(8,128)S(1)} %get-tuple-element.355, f32[4,256,128]{2,1,0:T(8,128)} %get-tuple-element.353, f32[4]{0:T(128)S(1)} %get-tuple-element.354, f32[4,256,128]{2,1,0:T(8,128)} %get-tuple-element.352, f32[4,256,128]{2,1,0:T(8,128)S(1)} %get-tuple-element.305, ...), kind=kLoop, calls=%fused_computation.15.clone.1 | loop fusion | flops 7602176 | bytes 3670032 | tf_op jit(solution)/shard_map/while/body/eval_jaxpr/reduce_sum | solution.py:87
  126.1 1.9 multiply_cosine_fusion.3
  128.0 9.7 %fusion.93 = (f32[256,4,128]{2,0,1:T(8,128)S(1)}, f32[256,4,128]{2,0,1:T(8,128)S(1)}) fusion(f32[4,256,128]{2,1,0:T(8,128)S(1)} %get-tuple-element.355, f32[4,256,128]{2,1,0:T(8,128)} %get-tuple-element.353, f32[4]{0:T(128)S(1)} %get-tuple-element.354, f32[4,256,128]{2,1,0:T(8,128)} %get-tuple-element.352, f32[4,256,128]{2,1,0:T(8,128)S(1)} %get-tuple-element.305, ...), kind=kLoop, calls=%fused_computation.15.clone.1 | loop fusion | flops 7602176 | bytes 3670032 | tf_op jit(solution)/shard_map/while/body/eval_jaxpr/reduce_sum | solution.py:87
  145.4 1.9 multiply_cosine_fusion.3
  147.3 9.7 %fusion.93 = (f32[256,4,128]{2,0,1:T(8,128)S(1)}, f32[256,4,128]{2,0,1:T(8,128)S(1)}) fusion(f32[4,256,128]{2,1,0:T(8,128)S(1)} %get-tuple-element.355, f32[4,256,128]{2,1,0:T(8,128)} %get-tuple-element.353, f32[4]{0:T(128)S(1)} %get-tuple-element.354, f32[4,256,128]{2,1,0:T(8,128)} %get-tuple-element.352, f32[4,256,128]{2,1,0:T(8,128)S(1)} %get-tuple-element.305, ...), kind=kLoop, calls=%fused_computation.15.clone.1 | loop fusion | flops 7602176 | bytes 3670032 | tf_op jit(solution)/shard_map/while/body/eval_jaxpr/reduce_sum | solution.py:87
  164.7 1.9 multiply_cosine_fusion.3
  166.6 9.7 %fusion.93 = (f32[256,4,128]{2,0,1:T(8,128)S(1)}, f32[256,4,128]{2,0,1:T(8,128)S(1)}) fusion(f32[4,256,128]{2,1,0:T(8,128)S(1)} %get-tuple-element.355, f32[4,256,128]{2,1,0:T(8,128)} %get-tuple-element.353, f32[4]{0:T(128)S(1)} %get-tuple-element.354, f32[4,256,128]{2,1,0:T(8,128)} %get-tuple-element.352, f32[4,256,128]{2,1,0:T(8,128)S(1)} %get-tuple-element.305, ...), kind=kLoop, calls=%fused_computation.15.clone.1 | loop fusion | flops 7602176 | bytes 3670032 | tf_op jit(solution)/shard_map/while/body/eval_jaxpr/reduce_sum | solution.py:87
  184.0 1.9 multiply_cosine_fusion.3
  185.9 9.7 %fusion.93 = (f32[256,4,128]{2,0,1:T(8,128)S(1)}, f32[256,4,128]{2,0,1:T(8,128)S(1)}) fusion(f32[4,256,128]{2,1,0:T(8,128)S(1)} %get-tuple-element.355, f32[4,256,128]{2,1,0:T(8,128)} %get-tuple-element.353, f32[4]{0:T(128)S(1)} %get-tuple-element.354, f32[4,256,128]{2,1,0:T(8,128)} %get-tuple-element.352, f32[4,256,128]{2,1,0:T(8,128)S(1)} %get-tuple-element.305, ...), kind=kLoop, calls=%fused_computation.15.clone.1 | loop fusion | flops 7602176 | bytes 3670032 | tf_op jit(solution)/shard_map/while/body/eval_jaxpr/reduce_sum | solution.py:87
  203.4 1.9 multiply_cosine_fusion.3
  205.2 9.7 %fusion.93 = (f32[256,4,128]{2,0,1:T(8,128)S(1)}, f32[256,4,128]{2,0,1:T(8,128)S(1)}) fusion(f32[4,256,128]{2,1,0:T(8,128)S(1)} %get-tuple-element.355, f32[4,256,128]{2,1,0:T(8,128)} %get-tuple-element.353, f32[4]{0:T(128)S(1)} %get-tuple-element.354, f32[4,256,128]{2,1,0:T(8,128)} %get-tuple-element.352, f32[4,256,128]{2,1,0:T(8,128)S(1)} %get-tuple-element.305, ...), kind=kLoop, calls=%fused_computation.15.clone.1 | loop fusion | flops 7602176 | bytes 3670032 | tf_op jit(solution)/shard_map/while/body/eval_jaxpr/reduce_sum | solution.py:87
  222.7 1.9 multiply_cosine_fusion.3
  224.5 9.7 %fusion.93 = (f32[256,4,128]{2,0,1:T(8,128)S(1)}, f32[256,4,128]{2,0,1:T(8,128)S(1)}) fusion(f32[4,256,128]{2,1,0:T(8,128)S(1)} %get-tuple-element.355, f32[4,256,128]{2,1,0:T(8,128)} %get-tuple-element.353, f32[4]{0:T(128)S(1)} %get-tuple-element.354, f32[4,256,128]{2,1,0:T(8,128)} %get-tuple-element.352, f32[4,256,128]{2,1,0:T(8,128)S(1)} %get-tuple-element.305, ...), kind=kLoop, calls=%fused_computation.15.clone.1 | loop fusion | flops 7602176 | bytes 3670032 | tf_op jit(solution)/shard_map/while/body/eval_jaxpr/reduce_sum | solution.py:87
  242.0 1.9 multiply_cosine_fusion.3
  243.9 9.7 %fusion.93 = (f32[256,4,128]{2,0,1:T(8,128)S(1)}, f32[256,4,128]{2,0,1:T(8,128)S(1)}) fusion(f32[4,256,128]{2,1,0:T(8,128)S(1)} %get-tuple-element.355, f32[4,256,128]{2,1,0:T(8,128)} %get-tuple-element.353, f32[4]{0:T(128)S(1)} %get-tuple-element.354, f32[4,256,128]{2,1,0:T(8,128)} %get-tuple-element.352, f32[4,256,128]{2,1,0:T(8,128)S(1)} %get-tuple-element.305, ...), kind=kLoop, calls=%fused_computation.15.clone.1 | loop fusion | flops 7602176 | bytes 3670032 | tf_op jit(solution)/shard_map/while/body/eval_jaxpr/reduce_sum | solution.py:87
  254.8 0.9 constant_dynamic-update-slice_fusion.6
  261.3 1.9 multiply_cosine_fusion.3
  263.2 9.7 %fusion.93 = (f32[256,4,128]{2,0,1:T(8,128)S(1)}, f32[256,4,128]{2,0,1:T(8,128)S(1)}) fusion(f32[4,256,128]{2,1,0:T(8,128)S(1)} %get-tuple-element.355, f32[4,256,128]{2,1,0:T(8,128)} %get-tuple-element.353, f32[4]{0:T(128)S(1)} %get-tuple-element.354, f32[4,256,128]{2,1,0:T(8,128)} %get-tuple-element.352, f32[4,256,128]{2,1,0:T(8,128)S(1)} %get-tuple-element.305, ...), kind=kLoop, calls=%fused_computation.15.clone.1 | loop fusion | flops 7602176 | bytes 3670032 | tf_op jit(solution)/shard_map/while/body/eval_jaxpr/reduce_sum | solution.py:87
  274.1 0.9 constant_dynamic-update-slice_fusion.6
  280.7 1.9 multiply_cosine_fusion.3
  282.5 9.7 %fusion.93 = (f32[256,4,128]{2,0,1:T(8,128)S(1)}, f32[256,4,128]{2,0,1:T(8,128)S(1)}) fusion(f32[4,256,128]{2,1,0:T(8,128)S(1)} %get-tuple-element.355, f32[4,256,128]{2,1,0:T(8,128)} %get-tuple-element.353, f32[4]{0:T(128)S(1)} %get-tuple-element.354, f32[4,256,128]{2,1,0:T(8,128)} %get-tuple-element.352, f32[4,256,128]{2,1,0:T(8,128)S(1)} %get-tuple-element.305, ...), kind=kLoop, calls=%fused_computation.15.clone.1 | loop fusion | flops 7602176 | bytes 3670032 | tf_op jit(solution)/shard_map/while/body/eval_jaxpr/reduce_sum | solution.py:87
  300.0 1.9 multiply_cosine_fusion.3
  301.8 9.7 %fusion.93 = (f32[256,4,128]{2,0,1:T(8,128)S(1)}, f32[256,4,128]{2,0,1:T(8,128)S(1)}) fusion(f32[4,256,128]{2,1,0:T(8,128)S(1)} %get-tuple-element.355, f32[4,256,128]{2,1,0:T(8,128)} %get-tuple-element.353, f32[4]{0:T(128)S(1)} %get-tuple-element.354, f32[4,256,128]{2,1,0:T(8,128)} %get-tuple-element.352, f32[4,256,128]{2,1,0:T(8,128)S(1)} %get-tuple-element.305, ...), kind=kLoop, calls=%fused_computation.15.clone.1 | loop fusion | flops 7602176 | bytes 3670032 | tf_op jit(solution)/shard_map/while/body/eval_jaxpr/reduce_sum | solution.py:87
  312.8 0.9 constant_dynamic-update-slice_fusion.6
  319.3 1.9 multiply_cosine_fusion.3
  321.2 9.7 %fusion.93 = (f32[256,4,128]{2,0,1:T(8,128)S(1)}, f32[256,4,128]{2,0,1:T(8,128)S(1)}) fusion(f32[4,256,128]{2,1,0:T(8,128)S(1)} %get-tuple-element.355, f32[4,256,128]{2,1,0:T(8,128)} %get-tuple-element.353, f32[4]{0:T(128)S(1)} %get-tuple-element.354, f32[4,256,128]{2,1,0:T(8,128)} %get-tuple-element.352, f32[4,256,128]{2,1,0:T(8,128)S(1)} %get-tuple-element.305, ...), kind=kLoop, calls=%fused_computation.15.clone.1 | loop fusion | flops 7602176 | bytes 3670032 | tf_op jit(solution)/shard_map/while/body/eval_jaxpr/reduce_sum | solution.py:87
  338.6 1.9 multiply_cosine_fusion.3
  340.5 9.7 %fusion.93 = (f32[256,4,128]{2,0,1:T(8,128)S(1)}, f32[256,4,128]{2,0,1:T(8,128)S(1)}) fusion(f32[4,256,128]{2,1,0:T(8,128)S(1)} %get-tuple-element.355, f32[4,256,128]{2,1,0:T(8,128)} %get-tuple-element.353, f32[4]{0:T(128)S(1)} %get-tuple-element.354, f32[4,256,128]{2,1,0:T(8,128)} %get-tuple-element.352, f32[4,256,128]{2,1,0:T(8,128)S(1)} %get-tuple-element.305, ...), kind=kLoop, calls=%fused_computation.15.clone.1 | loop fusion | flops 7602176 | bytes 3670032 | tf_op jit(solution)/shard_map/while/body/eval_jaxpr/reduce_sum | solution.py:87
  356.6 3.6 copy.51
  360.1 10.5 %pad_maximum_fusion.2 = f32[16,2,270,256]{2,3,1,0:T(8,128)} fusion(f32[16,2,14,256]{2,3,1,0:T(8,128)} %copy.51, f32[16,2,256,256]{2,3,1,0:T(8,128)} %get-tuple-element.53), kind=kLoop, calls=%fused_computation.41 | loop fusion | flops 2211840 | bytes 17694720 | tf_op jit(solution)/shard_map/concatenate | solution.py:38
  370.7 83.6 %reduce-scatter.2.cloned.1.call-done = f32[1,2,270,256]{2,3,1,0:T(8,128)} async-done(((f32[16,2,270,256]{2,3,1,0:T(8,128)}), f32[1,2,270,256]{2,3,1,0:T(8,128)}) %reduce-scatter.2.cloned.1.call-update) | async-done | bytes 552976 | tf_op jit(solution)/shard_map/reduce_scatter | solution.py:39
  454.2 1.0 slice_bitcast_fusion.2
  455.2 1.1 fusion.67
  456.9 11.7 %custom-call.38 = f32[1,128,128]{2,1,0:T(8,128)S(1)} custom-call(f32[1,128,128]{2,1,0:T(8,128)S(1)} %cholesky.267), custom_call_target="Cholesky" | custom-call | tf_op jit(solution)/shard_map/vmap(jit(cholesky))/cholesky | solution.py:57
  468.8 9.8 %custom-call.39 = f32[1,1,128,128]{2,3,1,0:T(8,128)S(1)} custom-call(f32[1,1,128,128]{3,2,1,0:T(8,128)S(1)} %get-tuple-element.196), custom_call_target="InvertDiagBlocksLowerTriangular" | custom-call | tf_op jit(solution)/shard_map/vmap(jit(cholesky))/cholesky | solution.py:57
  479.3 11.7 %custom-call.40 = f32[1,128,128]{2,1,0:T(8,128)S(1)} custom-call(f32[1,128,128]{2,1,0:T(8,128)S(1)} %cholesky.271), custom_call_target="Cholesky" | custom-call | tf_op jit(solution)/shard_map/vmap(jit(cholesky))/cholesky | solution.py:57
  491.0 9.9 %custom-call.41 = f32[1,1,128,128]{2,3,1,0:T(8,128)S(1)} custom-call(f32[1,1,128,128]{3,2,1,0:T(8,128)S(1)} %get-tuple-element.193), custom_call_target="InvertDiagBlocksLowerTriangular" | custom-call | tf_op jit(solution)/shard_map/vmap(jit(cholesky))/cholesky | solution.py:57
  501.6 11.7 %custom-call.42 = f32[1,128,128]{2,1,0:T(8,128)S(1)} custom-call(f32[1,128,128]{2,1,0:T(8,128)S(1)} %cholesky.276), custom_call_target="Cholesky" | custom-call | tf_op jit(solution)/shard_map/vmap(jit(cholesky))/cholesky | solution.py:57
  514.1 9.8 %custom-call.43 = f32[1,1,128,128]{2,3,1,0:T(8,128)S(1)} custom-call(f32[1,1,128,128]{3,2,1,0:T(8,128)S(1)} %get-tuple-element.190), custom_call_target="InvertDiagBlocksLowerTriangular" | custom-call | tf_op jit(solution)/shard_map/vmap(jit(cholesky))/cholesky | solution.py:57
  524.5 12.0 %custom-call.44 = f32[1,128,128]{2,1,0:T(8,128)S(1)} custom-call(f32[1,128,128]{2,1,0:T(8,128)S(1)} %fusion.35), custom_call_target="Cholesky" | custom-call | tf_op jit(solution)/shard_map/vmap(jit(cholesky))/cholesky | solution.py:57
  540.5 8.1 %while.15 = (s32[]{:T(128)}, f32[1,512,512]{2,1,0:T(8,128)S(1)}, s32[4,2]{0,1:T(2,128)S(1)}, f32[4,1,128,128]{3,2,1,0:T(8,128)S(1)}, s32[]{:T(128)}) while((s32[]{:T(128)}, f32[1,512,512]{2,1,0:T(8,128)S(1)}, s32[4,2]{0,1:T(2,128)S(1)}, f32[4,1,128,128]{3,2,1,0:T(8,128)S(1)}, s32[]{:T(128)}) %tuple.67), condition=%wide.while_cond, body=%wide.while_body.sunk | while | flops 2 | bytes 131181 | solution.py:58
  541.2 1.3 bitcast_dynamic-update-slice_fusion.2
  543.2 1.3 bitcast_dynamic-update-slice_fusion.2
  545.3 1.3 bitcast_dynamic-update-slice_fusion.2
  547.3 1.3 bitcast_dynamic-update-slice_fusion.2
  548.7 39.3 %custom-call.45 = f32[1,4,128,128]{2,3,1,0:T(8,128)S(1)} custom-call(f32[1,4,128,128]{3,2,1,0:T(8,128)S(1)} %bitcast.275), custom_call_target="InvertDiagBlocksLowerTriangular" | custom-call | tf_op jit(solution)/shard_map/vmap(jit(_cho_solve))/triangular_solve | solution.py:58
  588.0 1.0 slice_bitcast_fusion.17
  592.5 12.9 %all_to_all.10 = f32[16,1,2,14,256]{4,2,3,1,0:T(2,128)S(1)} all-to-all(f32[16,1,2,14,256]{4,2,3,1,0:T(2,128)S(1)} %broadcast_in_dim.66), channel_id=1, replica_groups=mesh['ap'=16,'sc'=8] {'ap'}, dimensions={0} | all-to-all | bytes 917504 | tf_op jit(solution)/shard_map/all_to_all | solution.py:14
  (282 shorter events, 85.7 us)
Async XLA Ops:
  9.1 36.2 %all-to-all-start = ((f32[8,16,32,128]{3,2,1,0:T(8,128)}), f32[8,16,32,128]{3,2,1,0:T(8,128)S(1)}, u32[]{:S(2)}, u32[]{:S(2)}) async-start(f32[8,16,32,128]{3,2,1,0:T(8,128)} %broadcast_in_dim.62), calls=%async_computation | async-start | bytes 4194304 | tf_op jit(solution)/shard_map/all_to_all | solution.py:14
  16.8 437.4 %reduce-scatter.2.cloned.1.call-start = ((), (), s32[]{:S(2)}) async-start(), calls=%async_computation.3 | async-start | bytes 13369344 | tf_op jit(solution)/shard_map/reduce_scatter | solution.py:39
  45.5 1.0 copy-start
  370.6 84.6 %copy-start.1 = (f32[256]{0:T(256)S(1)}, f32[256]{0:T(256)}, u32[]{:S(2)}) copy-start(f32[256]{0:T(256)} %param.15) | copy-start | bytes 3076
Sparse Core Ops, SparseCore 0:
  370.8 83.4 reduce-scatter.1
where the time goes:
time: 615 us; the launch traced here: 613 us
  other arithmetic  329 us (53%)
  waiting for transfers between devices  112 us (18%)
  local copies, waits for them, and re-layouts  65 us (11%)
  loops' own time  45.9 us (7%)
  matrix products  24.2 us (4%)
  between operations  16.2 us (3%)
  blocking collectives  12.9 us (2%)
  starting transfers between devices  7.76 us (1%)
    reduce_sum x16, other arithmetic, tone_responses(): jnp.sum(lead_re * turn_cos - lead_im * turn_sin, axis=0)  156 us
    reduce_scatter x1, waiting for transfers between devices, sent_together(): lax.psum_scatter(both, axis, scatter_dimension=dim, tiled=True)  83.6 us
    another operation x14, other arithmetic, solve_one(): factor = jnp.linalg.cholesky(system)  78.8 us
    another operation x1, loops' own time, on_device(): lax.map(tone_responses, jnp.arange(unit_response, dtype=jnp.int32))  45.8 us
    another operation x3, other arithmetic, solve_one(): solved = jax.scipy.linalg.cho_solve((factor, True), rhs)  39.4 us
    cos x16, other arithmetic, tone_responses(): turn_cos = jnp.cos(turn)[:, :, None, :]  30.1 us
    all_to_all x1, waiting for transfers between devices, copy_for_each(): lax.all_to_all(jnp.broadcast_to(value[None], (length, *value.shape)), axi...  28.4 us
    dynamic_update_slice x32, local copies, waits for them, and re-layouts, on_device(): lax.map(tone_responses, jnp.arange(unit_response, dtype=jnp.int32))  16.7 us
  transfers between devices with their start and end apart: 2, of which 2 were waited for; matrix products, arithmetic and copies ran while one was open for 0% of the time, Pallas kernels for 0%

commit v1 on v0

v1 whole, which is shorter than its diff:
```python
import functools
import math

import jax
import jax.numpy as jnp
import numpy as np
from jax import lax
from jax.experimental import pallas as pl
from jax.experimental.pallas import tpu as pltpu
from jax.sharding import PartitionSpec as P

CORES = 2
OWNERS = 8
Y_CHIPS = 4
Z_CHIPS = 2
X_CHIPS = 4
ANTENNAS = 4
PATHS = 4
FFT_LEN = 512
FIT_POINTS = 4001
ROWS = 16
HALF = 16
SOLVE_STEPS = 60
TOLERANCE = 2e-7


def turn_fit():
    u = 0.25 * np.cos(np.pi * (np.arange(FIT_POINTS) + 0.5) / FIT_POINTS)
    cheb = np.polynomial.chebyshev.Chebyshev
    poly = np.polynomial.Polynomial
    x = u * u
    fits = []
    for values, degree in ((np.sin(2 * np.pi * u) / u, 4), (np.cos(2 * np.pi * u), 5)):
        fits.append([float(c) for c in cheb.fit(x, values, degree, domain=[0, 0.0625]).convert(kind=poly).coef])
    return fits


SIN_FIT, COS_FIT = turn_fit()


def horner(x, coefs):
    total = jnp.full_like(x, coefs[-1])
    for c in coefs[-2::-1]:
        total = total * x + c
    return total


def small_turn(u):
    x = u * u
    return horner(x, COS_FIT), u * horner(x, SIN_FIT)


def doubled(c, s):
    return 1.0 - 2.0 * (s * s), 2.0 * (s * c)


def times(a, b):
    return a[0] * b[0] - a[1] * b[1], a[0] * b[1] + a[1] * b[0]


NT = (((1,), (1,)), ((), ()))


def product(a, b):
    return lax.dot_general(a, b, NT, preferred_element_type=jnp.float32)


def gram_kernel(place_ref, tone_ref, *refs):
    tab_refs, refs = refs[:OWNERS], refs[OWNERS:]
    count_ref, y_kept_ref, y_sent_ref, kept_ref, sent_ref, lead, step_turn, turn, hi, lo, received = refs
    pair = pl.program_id(0)
    users = count_ref.shape[0]
    per_block = tab_refs[0].shape[1]
    blocks = users // ROWS
    width = tab_refs[0].shape[2]
    half = ANTENNAS * width

    @pl.when(pair == 0)
    def _():
        centre = tone_ref[0]
        side = tone_ref[1]

        def prepare(slot, block, carry):
            tab_ref = tab_refs[slot]
            across, along = divmod(slot, X_CHIPS)
            owner = jnp.abs(place_ref[3] - across) * X_CHIPS + (place_ref[4] - along + X_CHIPS) % X_CHIPS
            inside = pl.ds(pl.multiple_of(block * ROWS, ROWS), ROWS)
            here = pl.ds(pl.multiple_of(owner * per_block + block * ROWS, ROWS), ROWS)
            count = count_ref[here, :]
            for p in range(PATHS):
                delay = tab_ref[p, inside, :]
                sine = tab_ref[PATHS + p, inside, :]
                alive = p < count
                re = jnp.where(alive, tab_ref[2 * PATHS + p, inside, :], 0.0)
                im = jnp.where(alive, tab_ref[3 * PATHS + p, inside, :], 0.0)
                half_step = small_turn(delay * (side * (0.5 / FFT_LEN)))
                turn[p, 0, here, :], turn[p, 1, here, :] = half_step
                step_turn[p, 0, here, :], step_turn[p, 1, here, :] = doubled(*half_step)
                turns = delay * centre
                turns = turns - jnp.round(turns)
                c, s = doubled(*small_turn(0.5 * turns))
                z = times((re, im), (c, -s))
                steer = doubled(*small_turn(0.25 * sine))
                for n in range(ANTENNAS):
                    lead[n, p, 0, here, :], lead[n, p, 1, here, :] = z
                    if n + 1 < ANTENNAS:
                        z = times(z, steer)
            return carry

        for slot in range(OWNERS):
            lax.fori_loop(0, per_block // ROWS, functools.partial(prepare, slot), 0)

    def build(block, carry):
        here = pl.ds(pl.multiple_of(block * ROWS, ROWS), ROWS)
        cs = [(turn[p, 0, here, :], turn[p, 1, here, :]) for p in range(PATHS)]
        for p in range(PATHS):
            turn[p, 0, here, :], turn[p, 1, here, :] = times(
                cs[p], (step_turn[p, 0, here, :], step_turn[p, 1, here, :])
            )
        for n in range(ANTENNAS):
            sums = None
            for p in range(PATHS):
                c, s = cs[p]
                re, im = lead[n, p, 0, here, :], lead[n, p, 1, here, :]
                four = (re * c, im * s, im * c, re * s)
                sums = four if sums is None else tuple(a + b for a, b in zip(sums, four))
            a, b, c, d = sums
            for tone, (re, im) in enumerate(((a - b, c + d), (a + b, c - d))):
                for start, value in ((n * width, re), (half + n * width, im)):
                    packed = value.astype(jnp.bfloat16)
                    hi[tone, here, start : start + width] = packed
                    lo[tone, here, start : start + width] = (value - packed.astype(jnp.float32)).astype(jnp.bfloat16)
        return carry

    lax.fori_loop(0, blocks, build, 0)
    for tone, (y_ref, out_ref) in enumerate(((y_sent_ref, sent_ref), (y_kept_ref, kept_ref))):
        y = y_ref[0]
        y_hi = y.astype(jnp.bfloat16)
        y_lo = (y - y_hi.astype(jnp.float32)).astype(jnp.bfloat16)
        received[...] = jnp.concatenate([y_hi, y_lo], 0)
        a = hi[tone]
        re, im = a[:, :half], a[:, half:]
        out_ref[0, :users, :] = product(a, a) + (product(re, im) - product(im, re))
        both = product(received[...], a)
        out_ref[0, users:, :] = both[: 2 * HALF] + both[2 * HALF :] + product(y_hi, lo[tone])


def tone_systems(place, centre, tables, counts, received):
    users, width = counts.shape
    tones = received.shape[0]
    wide = received.shape[2]
    pairs = tones // 2
    f32, bf16 = jnp.float32, jnp.bfloat16
    block = (1, users + 2 * HALF, users)

    def distance(j, place):
        along = (j % Y_CHIPS - place[2] + Y_CHIPS) % Y_CHIPS
        return (jnp.abs(j // Y_CHIPS - place[1]) * Y_CHIPS + along, 0, 0)

    grid_spec = pltpu.PrefetchScalarGridSpec(
        num_scalar_prefetch=1,
        grid=(pairs,),
        in_specs=[
            pl.BlockSpec(memory_space=pltpu.SMEM),
            *[pl.BlockSpec(t.shape, lambda j, place: (0, 0, 0), pipeline_mode=pl.Buffered(1)) for t in tables],
            pl.BlockSpec(counts.shape, lambda j, place: (0, 0), pipeline_mode=pl.Buffered(1)),
            pl.BlockSpec((1, 2 * HALF, wide), lambda j, place: (pairs - 1 - j + place[0] * (2 * j + 1), 0, 0)),
            pl.BlockSpec((1, 2 * HALF, wide), lambda j, place: (pairs + j - place[0] * (2 * j + 1), 0, 0)),
        ],
        out_specs=[pl.BlockSpec(block, distance)] * 2,
        scratch_shapes=[
            pltpu.VMEM((ANTENNAS, PATHS, 2, users, width), f32),
            pltpu.VMEM((PATHS, 2, users, width), f32),
            pltpu.VMEM((PATHS, 2, users, width), f32),
            pltpu.VMEM((2, users, wide), bf16),
            pltpu.VMEM((2, users, wide), bf16),
            pltpu.VMEM((4 * HALF, wide), bf16),
        ],
    )
    half = jax.ShapeDtypeStruct((pairs, users + 2 * HALF, users), f32)
    return pl.pallas_call(gram_kernel, grid_spec=grid_spec, out_shape=[half, half], name="tone_systems")(
        place, centre, *tables, counts, received, received
    )


def three_parts(x):
    hi = x.astype(jnp.bfloat16)
    rest = x - hi.astype(jnp.float32)
    mid = rest.astype(jnp.bfloat16)
    return hi, mid, (rest - mid.astype(jnp.float32)).astype(jnp.bfloat16)


def solve_kernel(*refs):
    *part_refs, regularizer_ref, out_ref, system_ref, parts, x_ref, r_ref, p_ref, work = refs
    system_ref[...] = sum(ref[0] for ref in part_refs)
    users = regularizer_ref.shape[1]
    f32 = jnp.float32
    g = system_ref[:users, :]
    flipped = g.T
    row = lax.broadcasted_iota(jnp.int32, (users, users), 0)
    column = lax.broadcasted_iota(jnp.int32, (users, users), 1)
    eye = row == column
    re = 0.5 * (g + flipped)
    im = 0.5 * (g - flipped)
    re = jnp.where(eye, re + regularizer_ref[...], re)
    diagonal = jnp.where(eye, re, 0.0)
    across = lax.rsqrt(jnp.sum(diagonal, 0, keepdims=True))
    down = lax.rsqrt(jnp.sum(diagonal, 1, keepdims=True))
    for k, matrix in enumerate((re, im)):
        for at, part in enumerate(three_parts(matrix * across * down)):
            parts[k, at] = part
    right = system_ref[users:, :] * across

    def together(v):
        total = jnp.sum(v[:HALF] + v[HALF:], 1, keepdims=True)
        return jnp.concatenate([total, total], 0)

    def dot(a, b):
        return jnp.dot(a, b, preferred_element_type=f32)

    rows = 2 * HALF

    def applied(p):
        hi, mid, low = three_parts(p)
        left3 = jnp.concatenate([hi, mid, low], 0)
        left2 = jnp.concatenate([hi, mid], 0)
        result = []
        for k in range(2):
            a = dot(left3, parts[k, 0])
            b = dot(left2, parts[k, 1])
            c = dot(hi, parts[k, 2])
            small = a[2 * rows :] + b[rows:] + c
            result.append(a[:rows] + ((a[rows : 2 * rows] + b[:rows]) + small))
        s, i = result
        return jnp.concatenate([s[:HALF] + i[HALF:], s[HALF:] - i[:HALF]], 0)

    norm = together(right * right)
    goal = norm * (TOLERANCE * TOLERANCE)
    x_ref[...] = jnp.zeros_like(right)
    r_ref[...] = right
    p_ref[...] = right

    def advance(state):
        done, _, rr = state
        for _ in range(2):
            p = p_ref[...]
            q = applied(p)
            pq = together(p * q)
            alpha = jnp.where(pq > 0.0, rr / pq, 0.0)
            x_ref[...] += alpha * p
            r = r_ref[...] - alpha * q
            r_ref[...] = r
            latest = together(r * r)
            p_ref[...] = r + jnp.where(rr > 0.0, latest / rr, 0.0) * p
            rr = latest
        return done + 2, jnp.max(jnp.where(rr <= goal, 0, 1)), rr

    def unfinished(state):
        done, left, _ = state
        return (left > 0) & (done < SOLVE_STEPS)

    _, left, _ = lax.while_loop(unfinished, advance, (0, jnp.max(jnp.where(norm <= goal, 0, 1)), norm))
    out_ref[...] = x_ref[...] * across

    @pl.when(left > 0)
    def _():
        work[0, :users, :] = re
        work[1, :users, :] = -im
        work[0, users:, :] = system_ref[users : users + HALF, :]
        work[1, users:, :] = system_ref[users + HALF :, :]
        lane = lax.broadcasted_iota(jnp.int32, (1, users), 1)

        def eliminate(j, carry):
            a, b = work[0], work[1]
            here = lane == j
            row_re = work[0, pl.ds(j, 1), :]
            row_im = work[1, pl.ds(j, 1), :]
            pivot = 1.0 / jnp.sum(jnp.where(here, row_re, 0.0), 1, keepdims=True)
            col_re = jnp.sum(jnp.where(here, a, 0.0), 1, keepdims=True) * pivot
            col_im = jnp.sum(jnp.where(here, b, 0.0), 1, keepdims=True) * pivot
            work[0] = jnp.where(here, col_re, a - (col_re * row_re - col_im * row_im))
            work[1] = jnp.where(here, col_im, b - (col_re * row_im + col_im * row_re))
            return carry

        lax.fori_loop(0, users, eliminate, 0)
        out_ref[:HALF, :] = work[0, users:, :]
        out_ref[HALF:, :] = work[1, users:, :]


def solved(systems, regularizer):
    _, rows, users = systems[0].shape
    f32 = jnp.float32
    vmem = pl.BlockSpec(memory_space=pltpu.VMEM)
    pair = pltpu.VMEM((2 * HALF, users), f32)
    return pl.pallas_call(
        solve_kernel,
        in_specs=[vmem] * (len(systems) + 1),
        out_specs=vmem,
        out_shape=jax.ShapeDtypeStruct((2 * HALF, users), f32),
        scratch_shapes=[
            pltpu.VMEM((rows, users), f32),
            pltpu.VMEM((2, 3, users, users), jnp.bfloat16),
            pair,
            pair,
            pair,
            pltpu.VMEM((2, users + HALF, users), f32),
        ],
        name="solved",
    )(*systems, regularizer.reshape(1, users))


def received_rows(observed_signal):
    _, samples, tones, antennas, width = observed_signal.shape
    y = jnp.moveaxis(observed_signal, 2, 0).reshape(tones, 2, samples, antennas * width)
    re, im = y[:, 0], y[:, 1]
    gap = ((0, 0), (0, HALF - samples), (0, 0))
    top = jnp.pad(jnp.concatenate([re, im], 2), gap)
    bottom = jnp.pad(jnp.concatenate([im, -re], 2), gap)
    return jnp.concatenate([top, bottom], 1)


def ap_at(z, y, core):
    return (z * Y_CHIPS + y % Y_CHIPS) * CORES + core


def over_ap(value, dz, dy, dcore):
    spots = [(z, y, c) for z in range(Z_CHIPS) for y in range(Y_CHIPS) for c in range(CORES)]
    pairs = [(ap_at(z, y, c), ap_at(z ^ dz, y + dy, c ^ dcore)) for z, y, c in spots]
    return lax.ppermute(value, "ap", pairs)


def over_sc(value, dz, dx):
    spots = [(z, x) for z in range(2) for x in range(X_CHIPS)]
    pairs = [(z * X_CHIPS + x, (z ^ dz) * X_CHIPS + (x + dx) % X_CHIPS) for z, x in spots]
    return lax.ppermute(value, "sc", pairs)


def gathered_tables(own):
    across = over_sc(own, 1, 0)
    near = [over_sc(own, 0, dx) for dx in (1, 2, 3)]
    far = [over_sc(across, 0, dx) for dx in (1, 2, 3)]
    return [own, *near, across, *far]


def on_device(observed_signal, delays, sines, path_gain_real, path_gain_imaginary, counts, regularizer):
    tones = observed_signal.shape[2]
    samples = observed_signal.shape[1]
    users = counts.shape[0]
    sc = lax.axis_index("sc")
    ap = lax.axis_index("ap")
    core = ap % CORES
    chip = ap // CORES
    place = jnp.stack([core, chip // Y_CHIPS, chip % Y_CHIPS, sc // X_CHIPS, sc % X_CHIPS]).astype(jnp.int32)
    first = (sc * tones).astype(jnp.float32)
    side = jnp.where(core == 0, -1.0, 1.0)
    centre = jnp.stack([(first + 0.5 * (tones - 1)) * (1.0 / FFT_LEN), side])
    own = jnp.concatenate([delays, sines, path_gain_real, path_gain_imaginary], 0)
    tables = gathered_tables(own)
    kept, sent = tone_systems(place, centre, tables, counts, received_rows(observed_signal))
    mine = kept + over_ap(sent, 0, 0, 1)
    steps = [(dz, dy) for dz in (1, 0) for dy in (2, 1, 3, 0) if dz or dy]
    parts = [over_ap(mine[dz * Y_CHIPS + dy][None], dz, dy, 0) for dz, dy in steps]
    own_tone = solved([mine[:1], *parts], regularizer)
    length = lax.axis_size("ap")
    every = lax.all_to_all(jnp.broadcast_to(own_tone[None], (length, *own_tone.shape)), "ap", 0, 0, tiled=True)
    every = every.reshape(length // CORES, CORES, 2, HALF, users)[:, :, :, :samples]
    every = jnp.concatenate([every[::-1, 0], every[:, 1]], 0)
    return jnp.transpose(every, (1, 2, 0, 3))


def solution(mesh):
    placed = (
        P(None, None, "sc", None, "ap"),
        P(None, "sc", "ap"),
        P(None, "sc", "ap"),
        P(None, "sc", "ap"),
        P(None, "sc", "ap"),
        P(None, "ap"),
        P(),
    )
    return jax.shard_map(
        on_device, mesh=mesh, in_specs=placed, out_specs=P(None, None, "sc", None), check_vma=False
    )
```

time: 615 us -> 135 us (0.22)
  other arithmetic: 329 us -> 4.59 us
  waiting for transfers between devices: 112 us -> 49 us
  local copies, waits for them, and re-layouts: 65 us -> 10.3 us
  loops' own time: 45.9 us -> 0 us
  Pallas kernels: 0 us -> 32.8 us
  matrix products: 24.2 us -> 0 us
  starting transfers between devices: 7.76 us -> 23.7 us
  between operations: 16.2 us -> 0.26 us
    reduce_sum x16 -> x0, other arithmetic: 156 us -> none  [tone_responses(): jnp.sum(lead_re * turn_cos - lead_im * turn_sin, axis=0)]
    another operation x51 -> x1, other arithmetic: 120 us -> 0.6 us  [on_device(): centre = jnp.stack([(first + 0.5 * (tones - 1)) * (1.0 / FFT_LEN), side])]
    reduce_scatter x1 -> x0, waiting for transfers between devices: 83.6 us -> none  [sent_together(): lax.psum_scatter(both, axis, scatter_dimension=dim, tiled=True)]
    ppermute x0 -> x15, waiting for transfers between devices: none -> 49 us  [the longest x8 34.2 us: over_ap(): return lax.ppermute(value, 'ap', pairs)]
    another operation x2 -> x0, loops' own time: 45.9 us -> none  [the longest x1 45.8 us: on_device(): lax.map(tone_responses, jnp.arange(unit_response, dtype=jnp.int32))]
    pallas_call x0 -> x2, Pallas kernels: none -> 32.8 us  [the longest x1 24.7 us: tone_systems(): pl.pallas_call(gram_kernel, grid_spec=grid_spec, out_shape=[half, half],...]
    cos x16 -> x0, other arithmetic: 30.1 us -> none  [tone_responses(): turn_cos = jnp.cos(turn)[:, :, None, :]]
    all_to_all x1 -> x0, waiting for transfers between devices: 28.4 us -> none  [copy_for_each(): lax.all_to_all(jnp.broadcast_to(value[None], (length, *value.shape)), axi...]
  transfers between devices with their start and end apart: 2 -> 15, of which waited for: 2 -> 9; matrix products, arithmetic and copies ran while one was open for 0% -> 4% of each run, Pallas kernels for 0% -> 0%
where the time goes in v1:
time: 135 us; the launch traced here: 134 us
  waiting for transfers between devices  49 us (36%)
  Pallas kernels  32.8 us (24%)
  starting transfers between devices  23.7 us (18%)
  blocking collectives  13.5 us (10%)
  local copies, waits for them, and re-layouts  10.3 us (8%)
  other arithmetic  4.59 us (3%)
    ppermute x8, waiting for transfers between devices, over_ap(): return lax.ppermute(value, 'ap', pairs)  34.2 us
    pallas_call x1, Pallas kernels, tone_systems(): pl.pallas_call(gram_kernel, grid_spec=grid_spec, out_shape=[half, half],...  24.7 us
    ppermute x7, waiting for transfers between devices, over_sc(): return lax.ppermute(value, 'sc', pairs)  14.8 us
    all_to_all x1, blocking collectives, on_device(): lax.all_to_all(jnp.broadcast_to(own_tone[None], (length, *own_tone.shape)...  13.5 us
    ppermute x7, starting transfers between devices, over_sc(): return lax.ppermute(value, 'sc', pairs)  12.4 us
    ppermute x8, starting transfers between devices, over_ap(): return lax.ppermute(value, 'ap', pairs)  11.3 us
    pallas_call x1, Pallas kernels, solved(): pl.pallas_call(solve_kernel, in_specs=[vmem] * (len(systems) + 1), out_sp...  8.15 us
    unnamed x34, local copies, waits for them, and re-layouts  4.01 us
  transfers between devices with their start and end apart: 15, of which 9 were waited for; matrix products, arithmetic and copies ran while one was open for 4% of the time, Pallas kernels for 0%

profile of v1, /device:TPU:0, one launch (start us, length us, event | category | flops | bytes accessed | tf_op | source)
XLA Modules:
  0.0 134.1 jit_solution(12311392980201639363)
XLA Ops:
  0.0 0.8 constant_dynamic-update-slice_fusion.3
  0.8 0.8 constant_dynamic-update-slice_fusion.2
  1.7 0.8 constant_dynamic-update-slice_fusion.1
  2.5 0.8 constant_dynamic-update-slice_fusion.refs_0_
  3.4 4.0 %collective-permute-start.3 = (f32[16,32,128]{2,1,0:T(8,128)S(1)}, f32[16,32,128]{2,1,0:T(8,128)S(1)}, u32[]{:S(2)}, u32[]{:S(2)}) collective-permute-start(f32[16,32,128]{2,1,0:T(8,128)S(1)} %constant_dynamic-update-slice_fusion.refs_0_), channel_id=1, source_target_pairs={{0,4},{1,5},{2,6},{3,7},{4,0},{5,1},{6,2},{7,3},{8,12},{9,13},{10,... | collective-permute-start | bytes 786440 | tf_op jit(solution)/shard_map/ppermute | solution.py:335
  7.4 2.8 %collective-permute-start.2 = (f32[16,32,128]{2,1,0:T(8,128)S(1)}, f32[16,32,128]{2,1,0:T(8,128)S(1)}, u32[]{:S(2)}, u32[]{:S(2)}) collective-permute-start(f32[16,32,128]{2,1,0:T(8,128)S(1)} %constant_dynamic-update-slice_fusion.refs_0_), channel_id=1, source_target_pairs={{0,3},{1,0},{2,1},{3,2},{4,7},{5,4},{6,5},{7,6},{8,11},{9,8},{10,9... | collective-permute-start | bytes 786440 | tf_op jit(solution)/shard_map/ppermute | solution.py:335
  10.1 0.8 collective-permute-start.1
  10.9 0.9 collective-permute-start
  11.8 1.5 %reshape.10 = f32[16,2,14,512]{3,0,2,1:T(8,128)S(1)} reshape(f32[16,2,14,4,128]{4,3,0,2,1:T(4,128)} %bitcast.27) | data formatting | bytes 1835008 | tf_op jit(solution)/shard_map/reshape | solution.py:314
  13.4 0.1 fusion.2
  13.4 0.5 copy_bitcast_fusion
  14.0 0.0 copy-done
  14.0 0.3 fusion
  14.4 0.6 stack.32.place_ref
  15.0 0.2 select_maximum_fusion.1
  15.1 0.0 collective-permute-done.3.refs_4_
  15.2 0.0 copy-start.8
  15.2 2.4 %collective-permute-start.6 = (f32[16,32,128]{2,1,0:T(8,128)S(1)}, f32[16,32,128]{2,1,0:T(8,128)S(1)}, u32[]{:S(2)}, u32[]{:S(2)}) collective-permute-start(f32[16,32,128]{2,1,0:T(8,128)S(1)} %collective-permute-done.3.refs_4_), channel_id=1, source_target_pairs={{0,3},{1,0},{2,1},{3,2},{4,7},{5,4},{6,5},{7,6},{8,11},{9,8},{10,9... | collective-permute-start | bytes 786440 | tf_op jit(solution)/shard_map/ppermute | solution.py:335
  17.6 1.5 %collective-permute-start.5 = (f32[16,32,128]{2,1,0:T(8,128)S(1)}, f32[16,32,128]{2,1,0:T(8,128)S(1)}, u32[]{:S(2)}, u32[]{:S(2)}) collective-permute-start(f32[16,32,128]{2,1,0:T(8,128)S(1)} %collective-permute-done.3.refs_4_), channel_id=1, source_target_pairs={{0,2},{1,3},{2,0},{3,1},{4,6},{5,7},{6,4},{7,5},{8,10},{9,11},{10,... | collective-permute-start | bytes 786440 | tf_op jit(solution)/shard_map/ppermute | solution.py:335
  19.1 3.0 %collective-permute-done.2.refs_3_ = f32[16,32,128]{2,1,0:T(8,128)S(1)} collective-permute-done((f32[16,32,128]{2,1,0:T(8,128)S(1)}, f32[16,32,128]{2,1,0:T(8,128)S(1)}, u32[]{:S(2)}, u32[]{:S(2)}) %collective-permute-start.2) | collective-permute-done | bytes 262176 | tf_op jit(solution)/shard_map/ppermute | solution.py:335
  22.1 0.0 collective-permute-start.4
  22.1 0.6 pad_maximum_fusion.1.tone_ref
  22.7 1.5 %pad_maximum_fusion.refs_9_.refs_10_ = f32[16,32,1024]{2,1,0:T(8,128)} fusion(f32[16,16,1024]{2,1,0:T(8,128)S(1)} %get-tuple-element.22, f32[16,16,1024]{2,1,0:T(8,128)S(1)} %get-tuple-element.21), kind=kLoop, calls=%fused_computation | loop fusion | flops 524288 | bytes 4194304 | tf_op jit(solution)/shard_map/concatenate | solution.py:319
  24.2 0.0 collective-permute-done.1.refs_2_
  24.2 2.3 %collective-permute-done.refs_1_ = f32[16,32,128]{2,1,0:T(8,128)S(1)} collective-permute-done((f32[16,32,128]{2,1,0:T(8,128)S(1)}, f32[16,32,128]{2,1,0:T(8,128)S(1)}, u32[]{:S(2)}, u32[]{:S(2)}) %collective-permute-start) | collective-permute-done | bytes 262176 | tf_op jit(solution)/shard_map/ppermute | solution.py:335
  26.5 5.8 %collective-permute-done.6.refs_7_ = f32[16,32,128]{2,1,0:T(8,128)S(1)} collective-permute-done((f32[16,32,128]{2,1,0:T(8,128)S(1)}, f32[16,32,128]{2,1,0:T(8,128)S(1)}, u32[]{:S(2)}, u32[]{:S(2)}) %collective-permute-start.6) | collective-permute-done | bytes 262176 | tf_op jit(solution)/shard_map/ppermute | solution.py:335
  32.3 0.0 collective-permute-done.5.refs_6_
  32.3 3.7 %collective-permute-done.4.refs_5_ = f32[16,32,128]{2,1,0:T(8,128)S(1)} collective-permute-done((f32[16,32,128]{2,1,0:T(8,128)S(1)}, f32[16,32,128]{2,1,0:T(8,128)S(1)}, u32[]{:S(2)}, u32[]{:S(2)}) %collective-permute-start.4) | collective-permute-done | bytes 262176 | tf_op jit(solution)/shard_map/ppermute | solution.py:335
  36.0 0.0 copy-done.8
  36.0 0.0 copy-done.9
  36.0 0.0 copy-done.10
  36.0 0.0 copy-done.11
  36.0 0.0 copy-done.12
  36.0 0.0 copy-done.13
  36.0 0.0 copy-start.14
  36.0 0.7 copy-done.14
  36.7 24.7 %tone_systems.1 = (f32[8,288,256]{2,1,0:T(8,128)}, f32[8,288,256]{2,1,0:T(8,128)}) custom-call(s32[5]{0:T(128)} %stack.32.place_ref, f32[2]{0:T(128)} %pad_maximum_fusion.1.tone_ref, f32[16,32,128]{2,1,0:T(8,128)} %copy-done, f32[16,32,128]{2,1,0:T(8,128)} %copy-done.11, f32[16,32,128]{2,1,0:T(8,128)} %copy-done.10, f32[16,32,128]{2,1,0:T(8,128)} %copy-done.9, ...), custom_call_target="tpu_custom_call" | custom-call | tf_op jit(solution)/shard_map/tone_systems/pallas_call | solution.py:181
  61.4 0.1 collective-permute-start.7
  61.5 4.7 %collective-permute-done.7 = f32[8,288,256]{2,1,0:T(8,128)S(1)} collective-permute-done((f32[8,288,256]{2,1,0:T(8,128)}, f32[8,288,256]{2,1,0:T(8,128)S(1)}, u32[]{:S(2)}, u32[]{:S(2)}) %collective-permute-start.7) | collective-permute-done | bytes 2359328 | tf_op jit(solution)/shard_map/ppermute | solution.py:329
  66.2 2.0 %add.27 = f32[8,288,256]{2,1,0:T(8,128)S(1)} add(f32[8,288,256]{2,1,0:T(8,128)} %get-tuple-element.7, f32[8,288,256]{2,1,0:T(8,128)S(1)} %collective-permute-done.7) | non-fusion elementwise | flops 589824 | bytes 7077888 | tf_op jit(solution)/shard_map/add | solution.py:360
  68.2 0.9 fusion.1
  69.1 3.0 %collective-permute-start.14 = (f32[1,288,256]{2,1,0:T(8,128)S(1)}, f32[1,288,256]{2,1,0:T(8,128)S(1)}, u32[]{:S(2)}, u32[]{:S(2)}) collective-permute-start(f32[1,288,256]{2,1,0:T(8,128)S(1)} %get-tuple-element.9), channel_id=1, source_target_pairs={{0,48},{8,56},{16,0},{24,8},{32,16},{40,24},{48,32},{56,40},{64,11... | collective-permute-start | bytes 884744 | tf_op jit(solution)/shard_map/ppermute | solution.py:329
  72.1 0.0 collective-permute-start.13
  72.1 2.2 %collective-permute-start.12 = (f32[1,288,256]{2,1,0:T(8,128)S(1)}, f32[1,288,256]{2,1,0:T(8,128)S(1)}, u32[]{:S(2)}, u32[]{:S(2)}) collective-permute-start(f32[1,288,256]{2,1,0:T(8,128)S(1)} %get-tuple-element.11), channel_id=1, source_target_pairs={{0,32},{8,40},{16,48},{24,56},{32,0},{40,8},{48,16},{56,24},{64,96... | collective-permute-start | bytes 884744 | tf_op jit(solution)/shard_map/ppermute | solution.py:329
  74.3 1.0 collective-permute-start.11
  75.3 1.5 %collective-permute-start.10 = (f32[1,288,256]{2,1,0:T(8,128)S(1)}, f32[1,288,256]{2,1,0:T(8,128)S(1)}, u32[]{:S(2)}, u32[]{:S(2)}) collective-permute-start(f32[1,288,256]{2,1,0:T(8,128)S(1)} %get-tuple-element.13), channel_id=1, source_target_pairs={{0,112},{8,120},{16,64},{24,72},{32,80},{40,88},{48,96},{56,104},{... | collective-permute-start | bytes 884744 | tf_op jit(solution)/shard_map/ppermute | solution.py:329
  76.8 9.0 %collective-permute-done.14.refs_7_ = f32[1,288,256]{2,1,0:T(8,128)S(1)} collective-permute-done((f32[1,288,256]{2,1,0:T(8,128)S(1)}, f32[1,288,256]{2,1,0:T(8,128)S(1)}, u32[]{:S(2)}, u32[]{:S(2)}) %collective-permute-start.14) | collective-permute-done | bytes 294944 | tf_op jit(solution)/shard_map/ppermute | solution.py:329
  85.8 0.0 collective-permute-start.9
  85.8 2.6 %collective-permute-done.13.refs_6_ = f32[1,288,256]{2,1,0:T(8,128)S(1)} collective-permute-done((f32[1,288,256]{2,1,0:T(8,128)S(1)}, f32[1,288,256]{2,1,0:T(8,128)S(1)}, u32[]{:S(2)}, u32[]{:S(2)}) %collective-permute-start.13) | collective-permute-done | bytes 294944 | tf_op jit(solution)/shard_map/ppermute | solution.py:329
  88.4 3.5 %collective-permute-start.8 = (f32[1,288,256]{2,1,0:T(8,128)S(1)}, f32[1,288,256]{2,1,0:T(8,128)S(1)}, u32[]{:S(2)}, u32[]{:S(2)}) collective-permute-start(f32[1,288,256]{2,1,0:T(8,128)S(1)} %get-tuple-element.15), channel_id=1, source_target_pairs={{0,96},{8,104},{16,112},{24,120},{32,64},{40,72},{48,80},{56,88},{... | collective-permute-start | bytes 884744 | tf_op jit(solution)/shard_map/ppermute | solution.py:329
  91.9 0.0 collective-permute-done.12.refs_5_
  91.9 0.0 collective-permute-done.11.refs_4_
  91.9 0.0 copy-start.4
  91.9 11.0 %collective-permute-done.10.refs_3_ = f32[1,288,256]{2,1,0:T(8,128)S(1)} collective-permute-done((f32[1,288,256]{2,1,0:T(8,128)S(1)}, f32[1,288,256]{2,1,0:T(8,128)S(1)}, u32[]{:S(2)}, u32[]{:S(2)}) %collective-permute-start.10) | collective-permute-done | bytes 294944 | tf_op jit(solution)/shard_map/ppermute | solution.py:329
  102.9 0.0 collective-permute-done.9.refs_2_
  102.9 6.9 %collective-permute-done.8.refs_1_ = f32[1,288,256]{2,1,0:T(8,128)S(1)} collective-permute-done((f32[1,288,256]{2,1,0:T(8,128)S(1)}, f32[1,288,256]{2,1,0:T(8,128)S(1)}, u32[]{:S(2)}, u32[]{:S(2)}) %collective-permute-start.8) | collective-permute-done | bytes 294944 | tf_op jit(solution)/shard_map/ppermute | solution.py:329
  109.8 0.0 copy-done.1
  109.8 0.0 copy-done.2
  109.8 0.0 copy-done.3
  109.9 0.7 copy-done.7
  110.5 8.1 %solved.1 = f32[32,256]{1,0:T(8,128)} custom-call(f32[1,288,256]{2,1,0:T(8,128)} %get-tuple-element.16.refs_0_, f32[1,288,256]{2,1,0:T(8,128)} %copy-done.7, f32[1,288,256]{2,1,0:T(8,128)} %copy-done.6, f32[1,288,256]{2,1,0:T(8,128)} %copy-done.5, f32[1,288,256]{2,1,0:T(8,128)} %copy-done.4, f32[1,288,256]{2,1,0:T(8,128)} %copy-done.3, ...), custom_call_target="tpu_custom_call" | custom-call | tf_op jit(solution)/shard_map/solved/pallas_call | solution.py:295
  118.7 0.8 broadcast_in_dim.2
  119.5 13.5 %all_to_all.5 = f32[16,32,256]{2,1,0:T(8,128)S(1)} all-to-all(f32[16,32,256]{2,1,0:T(8,128)S(1)} %broadcast_in_dim.2), channel_id=1, replica_groups=mesh['ap'=16,'sc'=8] {'ap'}, dimensions={0} | all-to-all | bytes 1048576 | tf_op jit(solution)/shard_map/all_to_all | solution.py:365
  133.1 1.0 copy.12
  (18 shorter events, 0.1 us)
Async XLA Ops:
  3.4 10.6 %copy-start = (f32[16,32,128]{2,1,0:T(8,128)}, f32[16,32,128]{2,1,0:T(8,128)S(1)}, u32[]{:S(2)}) copy-start(f32[16,32,128]{2,1,0:T(8,128)S(1)} %constant_dynamic-update-slice_fusion.refs_0_) | copy-start | bytes 786436
  3.4 11.8 %collective-permute-start.3 = (f32[16,32,128]{2,1,0:T(8,128)S(1)}, f32[16,32,128]{2,1,0:T(8,128)S(1)}, u32[]{:S(2)}, u32[]{:S(2)}) collective-permute-start(f32[16,32,128]{2,1,0:T(8,128)S(1)} %constant_dynamic-update-slice_fusion.refs_0_), channel_id=1, source_target_pairs={{0,4},{1,5},{2,6},{3,7},{4,0},{5,1},{6,2},{7,3},{8,12},{9,13},{10,... | collective-permute-start | bytes 786440 | tf_op jit(solution)/shard_map/ppermute | solution.py:335
  7.4 14.7 %collective-permute-start.2 = (f32[16,32,128]{2,1,0:T(8,128)S(1)}, f32[16,32,128]{2,1,0:T(8,128)S(1)}, u32[]{:S(2)}, u32[]{:S(2)}) collective-permute-start(f32[16,32,128]{2,1,0:T(8,128)S(1)} %constant_dynamic-update-slice_fusion.refs_0_), channel_id=1, source_target_pairs={{0,3},{1,0},{2,1},{3,2},{4,7},{5,4},{6,5},{7,6},{8,11},{9,8},{10,9... | collective-permute-start | bytes 786440 | tf_op jit(solution)/shard_map/ppermute | solution.py:335
  10.1 14.1 %collective-permute-start.1 = (f32[16,32,128]{2,1,0:T(8,128)S(1)}, f32[16,32,128]{2,1,0:T(8,128)S(1)}, u32[]{:S(2)}, u32[]{:S(2)}) collective-permute-start(f32[16,32,128]{2,1,0:T(8,128)S(1)} %constant_dynamic-update-slice_fusion.refs_0_), channel_id=1, source_target_pairs={{0,2},{1,3},{2,0},{3,1},{4,6},{5,7},{6,4},{7,5},{8,10},{9,11},{10,... | collective-permute-start | bytes 786440 | tf_op jit(solution)/shard_map/ppermute | solution.py:335
  10.9 15.6 %collective-permute-start = (f32[16,32,128]{2,1,0:T(8,128)S(1)}, f32[16,32,128]{2,1,0:T(8,128)S(1)}, u32[]{:S(2)}, u32[]{:S(2)}) collective-permute-start(f32[16,32,128]{2,1,0:T(8,128)S(1)} %constant_dynamic-update-slice_fusion.refs_0_), channel_id=1, source_target_pairs={{0,1},{1,2},{2,3},{3,0},{4,5},{5,6},{6,7},{7,4},{8,9},{9,10},{10,1... | collective-permute-start | bytes 786440 | tf_op jit(solution)/shard_map/ppermute | solution.py:335
  15.2 20.8 %copy-start.8 = (f32[16,32,128]{2,1,0:T(8,128)}, f32[16,32,128]{2,1,0:T(8,128)S(1)}, u32[]{:S(2)}) copy-start(f32[16,32,128]{2,1,0:T(8,128)S(1)} %collective-permute-done.3.refs_4_) | copy-start | bytes 786436
  15.2 17.1 %collective-permute-start.6 = (f32[16,32,128]{2,1,0:T(8,128)S(1)}, f32[16,32,128]{2,1,0:T(8,128)S(1)}, u32[]{:S(2)}, u32[]{:S(2)}) collective-permute-start(f32[16,32,128]{2,1,0:T(8,128)S(1)} %collective-permute-done.3.refs_4_), channel_id=1, source_target_pairs={{0,3},{1,0},{2,1},{3,2},{4,7},{5,4},{6,5},{7,6},{8,11},{9,8},{10,9... | collective-permute-start | bytes 786440 | tf_op jit(solution)/shard_map/ppermute | solution.py:335
  17.6 14.7 %collective-permute-start.5 = (f32[16,32,128]{2,1,0:T(8,128)S(1)}, f32[16,32,128]{2,1,0:T(8,128)S(1)}, u32[]{:S(2)}, u32[]{:S(2)}) collective-permute-start(f32[16,32,128]{2,1,0:T(8,128)S(1)} %collective-permute-done.3.refs_4_), channel_id=1, source_target_pairs={{0,2},{1,3},{2,0},{3,1},{4,6},{5,7},{6,4},{7,5},{8,10},{9,11},{10,... | collective-permute-start | bytes 786440 | tf_op jit(solution)/shard_map/ppermute | solution.py:335
  22.1 13.9 %copy-start.9 = (f32[16,32,128]{2,1,0:T(8,128)}, f32[16,32,128]{2,1,0:T(8,128)S(1)}, u32[]{:S(2)}) copy-start(f32[16,32,128]{2,1,0:T(8,128)S(1)} %collective-permute-done.2.refs_3_) | copy-start | bytes 786436
  22.1 13.9 %collective-permute-start.4 = (f32[16,32,128]{2,1,0:T(8,128)S(1)}, f32[16,32,128]{2,1,0:T(8,128)S(1)}, u32[]{:S(2)}, u32[]{:S(2)}) collective-permute-start(f32[16,32,128]{2,1,0:T(8,128)S(1)} %collective-permute-done.3.refs_4_), channel_id=1, source_target_pairs={{0,1},{1,2},{2,3},{3,0},{4,5},{5,6},{6,7},{7,4},{8,9},{9,10},{10,1... | collective-permute-start | bytes 786440 | tf_op jit(solution)/shard_map/ppermute | solution.py:335
  24.2 11.8 %copy-start.10 = (f32[16,32,128]{2,1,0:T(8,128)}, f32[16,32,128]{2,1,0:T(8,128)S(1)}, u32[]{:S(2)}) copy-start(f32[16,32,128]{2,1,0:T(8,128)S(1)} %collective-permute-done.1.refs_2_) | copy-start | bytes 786436
  26.5 9.4 %copy-start.11 = (f32[16,32,128]{2,1,0:T(8,128)}, f32[16,32,128]{2,1,0:T(8,128)S(1)}, u32[]{:S(2)}) copy-start(f32[16,32,128]{2,1,0:T(8,128)S(1)} %collective-permute-done.refs_1_) | copy-start | bytes 786436
  32.3 3.7 %copy-start.12 = (f32[16,32,128]{2,1,0:T(8,128)}, f32[16,32,128]{2,1,0:T(8,128)S(1)}, u32[]{:S(2)}) copy-start(f32[16,32,128]{2,1,0:T(8,128)S(1)} %collective-permute-done.6.refs_7_) | copy-start | bytes 786436
  32.3 3.7 %copy-start.13 = (f32[16,32,128]{2,1,0:T(8,128)}, f32[16,32,128]{2,1,0:T(8,128)S(1)}, u32[]{:S(2)}) copy-start(f32[16,32,128]{2,1,0:T(8,128)S(1)} %collective-permute-done.5.refs_6_) | copy-start | bytes 786436
  36.0 0.7 copy-start.14
  61.4 4.8 %collective-permute-start.7 = (f32[8,288,256]{2,1,0:T(8,128)}, f32[8,288,256]{2,1,0:T(8,128)S(1)}, u32[]{:S(2)}, u32[]{:S(2)}) collective-permute-start(f32[8,288,256]{2,1,0:T(8,128)} %get-tuple-element.8), channel_id=1, source_target_pairs={{0,8},{8,0},{16,24},{24,16},{32,40},{40,32},{48,56},{56,48},{64,72... | collective-permute-start | bytes 7077896 | tf_op jit(solution)/shard_map/ppermute | solution.py:329
  69.1 16.7 %collective-permute-start.14 = (f32[1,288,256]{2,1,0:T(8,128)S(1)}, f32[1,288,256]{2,1,0:T(8,128)S(1)}, u32[]{:S(2)}, u32[]{:S(2)}) collective-permute-start(f32[1,288,256]{2,1,0:T(8,128)S(1)} %get-tuple-element.9), channel_id=1, source_target_pairs={{0,48},{8,56},{16,0},{24,8},{32,16},{40,24},{48,32},{56,40},{64,11... | collective-permute-start | bytes 884744 | tf_op jit(solution)/shard_map/ppermute | solution.py:329
  72.1 16.3 %collective-permute-start.13 = (f32[1,288,256]{2,1,0:T(8,128)S(1)}, f32[1,288,256]{2,1,0:T(8,128)S(1)}, u32[]{:S(2)}, u32[]{:S(2)}) collective-permute-start(f32[1,288,256]{2,1,0:T(8,128)S(1)} %get-tuple-element.10), channel_id=1, source_target_pairs={{0,16},{8,24},{16,32},{24,40},{32,48},{40,56},{48,0},{56,8},{64,80... | collective-permute-start | bytes 884744 | tf_op jit(solution)/shard_map/ppermute | solution.py:329
  72.1 19.8 %collective-permute-start.12 = (f32[1,288,256]{2,1,0:T(8,128)S(1)}, f32[1,288,256]{2,1,0:T(8,128)S(1)}, u32[]{:S(2)}, u32[]{:S(2)}) collective-permute-start(f32[1,288,256]{2,1,0:T(8,128)S(1)} %get-tuple-element.11), channel_id=1, source_target_pairs={{0,32},{8,40},{16,48},{24,56},{32,0},{40,8},{48,16},{56,24},{64,96... | collective-permute-start | bytes 884744 | tf_op jit(solution)/shard_map/ppermute | solution.py:329
  74.3 17.6 %collective-permute-start.11 = (f32[1,288,256]{2,1,0:T(8,128)S(1)}, f32[1,288,256]{2,1,0:T(8,128)S(1)}, u32[]{:S(2)}, u32[]{:S(2)}) collective-permute-start(f32[1,288,256]{2,1,0:T(8,128)S(1)} %get-tuple-element.12), channel_id=1, source_target_pairs={{0,64},{8,72},{16,80},{24,88},{32,96},{40,104},{48,112},{56,120},{... | collective-permute-start | bytes 884744 | tf_op jit(solution)/shard_map/ppermute | solution.py:329
  75.3 27.6 %collective-permute-start.10 = (f32[1,288,256]{2,1,0:T(8,128)S(1)}, f32[1,288,256]{2,1,0:T(8,128)S(1)}, u32[]{:S(2)}, u32[]{:S(2)}) collective-permute-start(f32[1,288,256]{2,1,0:T(8,128)S(1)} %get-tuple-element.13), channel_id=1, source_target_pairs={{0,112},{8,120},{16,64},{24,72},{32,80},{40,88},{48,96},{56,104},{... | collective-permute-start | bytes 884744 | tf_op jit(solution)/shard_map/ppermute | solution.py:329
  85.8 24.0 %copy-start.1 = (f32[1,288,256]{2,1,0:T(8,128)}, f32[1,288,256]{2,1,0:T(8,128)S(1)}, u32[]{:S(2)}) copy-start(f32[1,288,256]{2,1,0:T(8,128)S(1)} %collective-permute-done.14.refs_7_) | copy-start | bytes 884740
  85.8 17.1 %collective-permute-start.9 = (f32[1,288,256]{2,1,0:T(8,128)S(1)}, f32[1,288,256]{2,1,0:T(8,128)S(1)}, u32[]{:S(2)}, u32[]{:S(2)}) collective-permute-start(f32[1,288,256]{2,1,0:T(8,128)S(1)} %get-tuple-element.14), channel_id=1, source_target_pairs={{0,80},{8,88},{16,96},{24,104},{32,112},{40,120},{48,64},{56,72},{... | collective-permute-start | bytes 884744 | tf_op jit(solution)/shard_map/ppermute | solution.py:329
  88.4 21.4 %copy-start.2 = (f32[1,288,256]{2,1,0:T(8,128)}, f32[1,288,256]{2,1,0:T(8,128)S(1)}, u32[]{:S(2)}) copy-start(f32[1,288,256]{2,1,0:T(8,128)S(1)} %collective-permute-done.13.refs_6_) | copy-start | bytes 884740
  88.4 21.4 %collective-permute-start.8 = (f32[1,288,256]{2,1,0:T(8,128)S(1)}, f32[1,288,256]{2,1,0:T(8,128)S(1)}, u32[]{:S(2)}, u32[]{:S(2)}) collective-permute-start(f32[1,288,256]{2,1,0:T(8,128)S(1)} %get-tuple-element.15), channel_id=1, source_target_pairs={{0,96},{8,104},{16,112},{24,120},{32,64},{40,72},{48,80},{56,88},{... | collective-permute-start | bytes 884744 | tf_op jit(solution)/shard_map/ppermute | solution.py:329
  91.9 18.0 %copy-start.3 = (f32[1,288,256]{2,1,0:T(8,128)}, f32[1,288,256]{2,1,0:T(8,128)S(1)}, u32[]{:S(2)}) copy-start(f32[1,288,256]{2,1,0:T(8,128)S(1)} %collective-permute-done.12.refs_5_) | copy-start | bytes 884740
  91.9 18.0 %copy-start.4 = (f32[1,288,256]{2,1,0:T(8,128)}, f32[1,288,256]{2,1,0:T(8,128)S(1)}, u32[]{:S(2)}) copy-start(f32[1,288,256]{2,1,0:T(8,128)S(1)} %collective-permute-done.11.refs_4_) | copy-start | bytes 884740
  102.9 7.0 %copy-start.5 = (f32[1,288,256]{2,1,0:T(8,128)}, f32[1,288,256]{2,1,0:T(8,128)S(1)}, u32[]{:S(2)}) copy-start(f32[1,288,256]{2,1,0:T(8,128)S(1)} %collective-permute-done.10.refs_3_) | copy-start | bytes 884740
  102.9 7.0 %copy-start.6 = (f32[1,288,256]{2,1,0:T(8,128)}, f32[1,288,256]{2,1,0:T(8,128)S(1)}, u32[]{:S(2)}) copy-start(f32[1,288,256]{2,1,0:T(8,128)S(1)} %collective-permute-done.9.refs_2_) | copy-start | bytes 884740
  109.8 0.7 copy-start.7
